TPU v7x, 128 devices: a whole 4x4x4 slice. The times are simulated.
128 devices in a mesh: group: 8 (over z, core), member: 16 (over x, y).
Axes of the slice: x: 4, y: 4, z: 4, core: 2. Of those that a mesh axis runs over, the one named last changes fastest.
Arguments:
- hidden: bfloat16 [12288, 2048], P('group'), may hold values from -6 to 6
- token_slab: int32 [12288, 1], P(('group', 'member')), may hold values from 0 to 127; in each aligned block of 96 rows (0 to 95, 96 to 191, ...) at most 2 rows name the same one
- token_row: int32 [12288], P(('group', 'member')), may hold values from 0 to 2047
- slab_owner: int32 [128], replicated, may hold values from 0 to 127, each once
- ple_table: bfloat16 [262144, 256], P(('group', 'member')), may hold values from -0.375 to 0.375
- norm_gains: float32 [1, 3, 2048], replicated, may hold values from 0.1 to 1.9
- w_gate: bfloat16 [1, 2048, 8192], P(None, None, 'member'), may hold values from -0.125 to 0.125
- w_up: bfloat16 [1, 2048, 8192], P(None, None, 'member'), may hold values from -0.125 to 0.125
- w_down: bfloat16 [1, 8192, 2048], P(None, 'member'), may hold values from -0.0625 to 0.0625
- ple_gate: bfloat16 [1, 2048, 256], P(None, None, 'member'), may hold values from -0.125 to 0.125
- ple_proj: bfloat16 [1, 256, 2048], P(None, 'member'), may hold values from -0.375 to 0.375
Outputs:
- hidden_out: bfloat16 [12288, 2048], P('group')
Inputs may be any that keep to these rules, and one draw needn't show every extreme that they name: Within the 96 tokens of one device (aligned blocks of token_slab), no slab is named by more than 2 tokens. Each number appears once: slab s is stored in rows slab_owner[s] * 2048 to slab_owner[s] * 2048 + 2047 of ple_table.
All inputs are finite; a program needn't handle non-finite values.
Results may differ from a plain program's by a relative error of at most 0.0061.
Values may be sent and summed in bfloat16 or wider, within the bound.
A program may use at most 128 MiB of HBM per device.

v0:
```python
import jax
import jax.numpy as jnp
from jax import lax
from jax.sharding import PartitionSpec as P

PLE = 256
epsilon = 1e-06


def norm_rows(values, scales):
    return values * lax.rsqrt(jnp.mean(values * values, axis=-1, keepdims=True) + epsilon) * scales


def per_device(
    hidden,
    token_slab,
    token_row,
    slab_owner,
    ple_table,
    norm_gains,
    w_gate,
    w_up,
    w_down,
    ple_gate,
    ple_proj,
):
    members = lax.axis_size("member")
    devices = lax.axis_size("group") * members
    tokens_here = token_row.shape[0]
    slots = max(2, (2 * tokens_here + devices - 1) // devices)
    me = lax.axis_index("member")
    gate_full = lax.all_gather(ple_gate[0].T, "member", axis=0, tiled=True)
    proj_full = lax.all_gather(ple_proj[0], "member", axis=0, tiled=True)
    normed = norm_rows(hidden.astype(jnp.float32), norm_gains[0, 0]).astype(jnp.bfloat16)
    gate_part = jnp.dot(normed, w_gate[0], preferred_element_type=jnp.float32)
    up_part = jnp.dot(normed, w_up[0], preferred_element_type=jnp.float32)
    activated = (jax.nn.gelu(gate_part, approximate=True) * up_part).astype(jnp.bfloat16)
    partial = jnp.dot(activated, w_down[0], preferred_element_type=jnp.float32).astype(jnp.bfloat16)
    mlp_out = lax.psum_scatter(partial, "member", scatter_dimension=0, tiled=True).astype(
        jnp.float32
    )
    target = slab_owner[token_slab[:, 0]]
    order = jnp.arange(tokens_here, dtype=jnp.int32)
    earlier = (target[None, :] == target[:, None]) & (order[None, :] < order[:, None])
    slot_of = jnp.sum(earlier.astype(jnp.int32), axis=1)
    hit_map = (target[:, None, None] == jnp.arange(devices, dtype=jnp.int32)[None, :, None]) & (
        slot_of[:, None, None] == jnp.arange(slots, dtype=jnp.int32)[None, None, :]
    )
    requests = jnp.sum(jnp.where(hit_map, token_row[:, None, None] + 1, 0), axis=0)
    received = lax.all_to_all(
        requests, ("group", "member"), split_axis=0, concat_axis=0, tiled=True
    )
    flat_ids = received.reshape(-1) - 1
    one_hot = (
        flat_ids[:, None] == jnp.arange(ple_table.shape[0], dtype=jnp.int32)[None, :]
    ).astype(jnp.bfloat16)
    served = jnp.dot(one_hot, ple_table, preferred_element_type=jnp.float32).astype(jnp.bfloat16)
    served = served.reshape(devices, slots * ple_table.shape[1])
    returned = lax.all_to_all(served, ("group", "member"), split_axis=0, concat_axis=0, tiled=True)
    returned = returned.reshape(devices * slots, ple_table.shape[1])
    own_rows = jnp.dot(
        hit_map.reshape(tokens_here, devices * slots).astype(jnp.bfloat16),
        returned,
        preferred_element_type=jnp.float32,
    )
    mine = lax.dynamic_slice_in_dim(hidden, me * tokens_here, tokens_here, 0).astype(jnp.float32)
    current = mine + norm_rows(mlp_out, norm_gains[0, 1])
    current_b = current.astype(jnp.bfloat16)
    gate_out = lax.dot_general(
        current_b, gate_full, (((1,), (1,)), ((), ())), preferred_element_type=jnp.float32
    )
    ple_act = (jax.nn.gelu(gate_out, approximate=True) * (own_rows * PLE**0.5)).astype(jnp.bfloat16)
    ple_out = jnp.dot(ple_act, proj_full, preferred_element_type=jnp.float32)
    current = current + norm_rows(ple_out, norm_gains[0, 2])
    return lax.all_gather(current.astype(jnp.bfloat16), "member", axis=0, tiled=True)


def solution(mesh):
    return jax.shard_map(
        per_device,
        mesh=mesh,
        in_specs=(
            P("group", None),
            P(("group", "member"), None),
            P(("group", "member")),
            P(),
            P(("group", "member"), None),
            P(),
            P(None, None, "member"),
            P(None, None, "member"),
            P(None, "member", None),
            P(None, None, "member"),
            P(None, "member", None),
        ),
        out_specs=P("group", None),
        check_vma=False,
    )
```

profile of v0, /device:TPU:1, one launch (start us, length us, event | category | flops | bytes accessed | tf_op | source)
XLA Modules:
  0.0 283.0 jit_solution(1658720977791138758)
XLA Ops:
  6.5 4.2 %fusion = f32[1536]{0:T(1024)S(1)} fusion(bf16[1536,2048]{1,0:T(8,128)(2,1)} %param.11), kind=kLoop, calls=%fused_computation.3 | loop fusion | flops 9435648 | bytes 6297600 | tf_op jit(solution)/shard_map/reduce_sum | solution.py:11
  10.8 0.5 copy-done.2
  11.3 6.8 %fusion.13 = f32[1536,512]{1,0:T(8,128)} fusion(bf16[1,2048,512]{2,1,0:T(8,128)(2,1)} %param.17, bf16[1536,2048]{1,0:T(8,128)(2,1)S(1)} %copy-done.2, f32[2048]{0:T(1024)S(1)} %bitcast.36, f32[1536]{0:T(1024)S(1)} %add_rsqrt_fusion), kind=kOutput, calls=%fused_computation.19 | convolution fusion | flops 3233808384 | bytes 11548672 | tf_op jit(solution)/shard_map/dot_general | solution.py:35
  18.1 12.4 %convolution_convert_fusion = bf16[1536,2048]{1,0:T(8,128)(2,1)} fusion(bf16[1,512,2048]{2,1,0:T(8,128)(2,1)S(1)} %copy-done, f32[1536,512]{1,0:T(8,128)} %fusion.13, bf16[1,2048,512]{2,1,0:T(8,128)(2,1)} %param.18, bf16[1536,2048]{1,0:T(8,128)(2,1)} %param.11, f32[2048]{0:T(1024)S(1)} %bitcast.37, f32[1536]{0:T(1024)S(1)} %add_rsqrt_fusion), kind=kOutput, calls=%fused_computation.6 | convolution fusion | flops 6466043904 | bytes 19937280 | tf_op jit(solution)/shard_map/dot_general | solution.py:38
  30.6 0.7 all-gather.5.cloned.1.call-update
  31.3 0.7 all-gather.9.cloned.1.call-update
  32.1 1.2 gather_fusion
  33.3 0.2 convert_reduce_fusion
  33.5 2.2 select_reduce_fusion
  35.8 21.2 %all_to_all.19 = s32[128,1,2]{2,1,0:T(1,128)S(1)} all-to-all(s32[128,1,2]{2,1,0:T(1,128)S(1)} %bitcast.31), channel_id=1, replica_groups=mesh['group'=8,'member'=16] {'group','member'}, dimensions={0} | all-to-all | bytes 2048 | tf_op jit(solution)/shard_map/all_to_all | solution.py:50
  56.9 0.2 add_reduce_fusion
  57.1 0.1 sub.7
  57.2 1.7 fusion.22
  59.0 0.1 all_to_all.16
  59.0 0.6 broadcast.109
  59.6 1.4 reduce.5
  61.0 0.7 reshape.127
  61.7 4.4 %all-to-all-start.1 = ((bf16[128,2,256]{2,1,0:T(2,128)(2,1)}), bf16[128,2,256]{2,1,0:T(2,128)(2,1)S(1)}, u32[]{:S(2)}, u32[]{:S(2)}) async-start(bf16[128,2,256]{2,1,0:T(2,128)(2,1)} %reshape.127), calls=%async_computation.2 | async-start | bytes 262144 | tf_op jit(solution)/shard_map/all_to_all | solution.py:59
  66.1 0.1 and.31
  66.2 10.9 %all-to-all-done.1 = bf16[128,2,256]{2,1,0:T(2,128)(2,1)S(1)} async-done(((bf16[128,2,256]{2,1,0:T(2,128)(2,1)}), bf16[128,2,256]{2,1,0:T(2,128)(2,1)S(1)}, u32[]{:S(2)}, u32[]{:S(2)}) %all-to-all-start.1) | async-done | bytes 131104 | tf_op jit(solution)/shard_map/all_to_all | solution.py:59
  77.1 0.1 reshape.128
  77.2 0.8 reduce.1
  78.1 36.8 %reduce-scatter.2.cloned.1.call-done = bf16[96,2048]{1,0:T(8,128)(2,1)} async-done(((bf16[1536,2048]{1,0:T(8,128)(2,1)}), bf16[96,2048]{1,0:T(8,128)(2,1)}) %reduce-scatter.2.cloned.1.call-update) | async-done | bytes 393232 | tf_op jit(solution)/shard_map/reduce_scatter | solution.py:39
  114.9 1.2 fusion.28
  116.2 42.5 %all-gather.5.cloned.1.call-done = bf16[256,2048]{1,0:T(8,128)(2,1)} async-done(((bf16[16,2048]{1,0:T(8,128)(2,1)}), bf16[256,2048]{1,0:T(8,128)(2,1)}) %all-gather.5.cloned.1.call-update) | async-done | bytes 1048592 | tf_op jit(solution)/shard_map/all_gather | solution.py:32
  158.7 2.0 fusion.43
  160.6 42.0 %all-gather.9.cloned.1.call-done = bf16[1,256,2048]{2,1,0:T(8,128)(2,1)} async-done(((bf16[1,16,2048]{2,1,0:T(8,128)(2,1)}), bf16[1,256,2048]{2,1,0:T(8,128)(2,1)}) %all-gather.9.cloned.1.call-update) | async-done | bytes 1048592 | tf_op jit(solution)/shard_map/all_gather | solution.py:33
  202.7 2.3 multiply_reduce_fusion
  205.0 0.7 add_rsqrt_fusion.1
  205.7 2.1 add_convert_fusion
  207.8 62.1 %all-gather.7.cloned.1.call-done = bf16[1536,2048]{1,0:T(8,128)(2,1)} async-done(((bf16[96,2048]{1,0:T(8,128)(2,1)}), bf16[1536,2048]{1,0:T(8,128)(2,1)}) %all-gather.7.cloned.1.call-update) | async-done | bytes 6291472 | tf_op jit(solution)/shard_map/all_gather | solution.py:75
  269.9 6.6 %copy.17 = bf16[1536,2048]{1,0:T(8,128)(2,1)} copy(bf16[1536,2048]{1,0:T(8,128)(2,1)} %all-gather.7.cloned.1.call-done) | data formatting | bytes 12582912
  (30 shorter events, 0.3 us)
Async XLA Ops:
  6.5 11.6 %copy-start = (bf16[1,512,2048]{2,1,0:T(8,128)(2,1)S(1)}, bf16[1,512,2048]{2,1,0:T(8,128)(2,1)}, u32[]{:S(2)}) copy-start(bf16[1,512,2048]{2,1,0:T(8,128)(2,1)} %param.19) | copy-start | bytes 6291460
  6.5 4.3 %copy-start.4 = (f32[1,3,2048]{2,0,1:T(1,128)S(1)}, f32[1,3,2048]{2,0,1:T(1,128)}, u32[]{:S(2)}) copy-start(f32[1,3,2048]{2,0,1:T(1,128)} %param.16) | copy-start | bytes 73732
  6.5 108.4 %reduce-scatter.2.cloned.1.call-start = ((), (), s32[]{:S(2)}) async-start(), calls=%async_computation.3 | async-start | bytes 6684672 | tf_op jit(solution)/shard_map/reduce_scatter | solution.py:39
  6.5 4.8 %copy-start.2 = (bf16[1536,2048]{1,0:T(8,128)(2,1)S(1)}, bf16[1536,2048]{1,0:T(8,128)(2,1)}, u32[]{:S(2)}) copy-start(bf16[1536,2048]{1,0:T(8,128)(2,1)} %param.11) | copy-start | bytes 18874372
  30.5 1.5 copy-start.6
  30.5 1.5 copy-start.7
  30.5 1.6 copy-start.1
  30.5 128.1 %all-gather.5.cloned.1.call-start = ((), (), s32[]{:S(2)}) async-start(), calls=%async_computation.4 | async-start | bytes 1114112 | tf_op jit(solution)/shard_map/all_gather | solution.py:32
  31.3 171.4 %all-gather.9.cloned.1.call-start = ((), (), s32[]{:S(2)}) async-start(), calls=%async_computation.6 | async-start | bytes 1114112 | tf_op jit(solution)/shard_map/all_gather | solution.py:33
  61.7 15.5 %all-to-all-start.1 = ((bf16[128,2,256]{2,1,0:T(2,128)(2,1)}), bf16[128,2,256]{2,1,0:T(2,128)(2,1)S(1)}, u32[]{:S(2)}, u32[]{:S(2)}) async-start(bf16[128,2,256]{2,1,0:T(2,128)(2,1)} %reshape.127), calls=%async_computation.2 | async-start | bytes 262144 | tf_op jit(solution)/shard_map/all_to_all | solution.py:59
  66.1 203.8 %all-gather.7.cloned.1.call-start = ((), (), s32[]{:S(2)}) async-start(), calls=%async_computation.5 | async-start | bytes 6684672 | tf_op jit(solution)/shard_map/all_gather | solution.py:75
  114.9 90.8 %copy-start.3 = (bf16[96,2048]{1,0:T(8,128)(2,1)S(1)}, bf16[96,2048]{1,0:T(8,128)(2,1)}, u32[]{:S(2)}) copy-start(bf16[96,2048]{1,0:T(8,128)(2,1)} %reduce-scatter.2.cloned.1.call-done) | copy-start | bytes 1179652
  116.2 44.5 %copy-start.5 = (f32[96]{0:T(128)}, f32[96]{0:T(128)S(1)}, u32[]{:S(2)}) copy-start(f32[96]{0:T(128)S(1)} %add_rsqrt_fusion.2) | copy-start | bytes 1156
Sparse Core Ops, SparseCore 0:
  30.6 84.2 reduce-scatter.1
  117.0 41.5 all-gather.4
  160.8 41.8 all-gather.8
  207.9 61.9 all-gather.6
where the time goes:
time: 283 us
  waiting for transfers between devices  196 us (69%)
  matrix products  25.2 us (9%)
  blocking collectives  21.2 us (7%)
  between operations  13.3 us (5%)
  other arithmetic  13 us (5%)
  local copies, waits for them, and re-layouts  10 us (4%)
  starting transfers between devices  4.54 us (2%)
    all_gather x1, waiting for transfers between devices, per_device(): lax.all_gather(current.astype(jnp.bfloat16), 'member', axis=0, tiled=True)  62.1 us
    all_gather x1, waiting for transfers between devices, per_device(): gate_full = lax.all_gather(ple_gate[0].T, 'member', axis=0, tiled=True)  42.5 us
    all_gather x1, waiting for transfers between devices, per_device(): proj_full = lax.all_gather(ple_proj[0], 'member', axis=0, tiled=True)  42 us
    reduce_scatter x1, waiting for transfers between devices, per_device(): lax.psum_scatter(partial, 'member', scatter_dimension=0, tiled=True)  36.8 us
    all_to_all x1, blocking collectives, per_device(): lax.all_to_all(requests, ('group', 'member'), split_axis=0, concat_axis=0...  21.2 us
    dot_general x1, matrix products, per_device(): jnp.dot(activated, w_down[0], preferred_element_type=jnp.float32)  12.4 us
    all_to_all x1, waiting for transfers between devices, per_device(): lax.all_to_all(served, ('group', 'member'), split_axis=0, concat_axis=0,...  10.9 us
    unnamed x19, local copies, waits for them, and re-layouts  7.92 us
  transfers between devices with their start and end apart: 5, of which 5 were waited for; matrix products, arithmetic and copies ran while one was open for 4% of the time, Pallas kernels for 0%

commit v1 on v0

--- a/solution.py
+++ b/solution.py
@@ -29,7 +29,11 @@
     tokens_here = token_row.shape[0]
     slots = max(2, (2 * tokens_here + devices - 1) // devices)
     me = lax.axis_index("member")
-    gate_full = lax.all_gather(ple_gate[0].T, "member", axis=0, tiled=True)
+    part = ple_gate[0].T
+    size = lax.axis_size("member")
+    blocks = jnp.stack([part for _ in range(size)])
+    blocks = lax.all_to_all(blocks, "member", split_axis=0, concat_axis=0)
+    gate_full = jnp.concatenate(blocks, axis=0)
     proj_full = lax.all_gather(ple_proj[0], "member", axis=0, tiled=True)
     normed = norm_rows(hidden.astype(jnp.float32), norm_gains[0, 0]).astype(jnp.bfloat16)
     gate_part = jnp.dot(normed, w_gate[0], preferred_element_type=jnp.float32)

time: 283 us -> 246 us (0.87)
  waiting for transfers between devices: 196 us -> 142 us
  blocking collectives: 21.2 us -> 35.7 us
    all_gather x1 -> x0, waiting for transfers between devices: 42.5 us -> none  [per_device(): gate_full = lax.all_gather(ple_gate[0].T, 'member', axis=0, tiled=True)]
    all_to_all x0 -> x1, blocking collectives: none -> 14.6 us  [per_device(): lax.all_to_all(served, ('group', 'member'), split_axis=0, concat_axis=0,...]
    all_to_all x1, waiting for transfers between devices: 10.9 us -> 0.01 us  [per_device(): blocks = lax.all_to_all(blocks, 'member', split_axis=0, concat_axis=0)]
  transfers between devices with their start and end apart: 5 -> 4, of which waited for: 5 -> 3; matrix products, arithmetic and copies ran while one was open for 4% -> 7% of each run, Pallas kernels for 0% -> 0%
where the time goes in v1:
time: 246 us
  waiting for transfers between devices  142 us (58%)
  blocking collectives  35.7 us (15%)
  matrix products  25.1 us (10%)
  other arithmetic  13.4 us (5%)
  between operations  13.3 us (5%)
  local copies, waits for them, and re-layouts  12.7 us (5%)
  starting transfers between devices  3.74 us (2%)
    all_gather x1, waiting for transfers between devices, per_device(): lax.all_gather(current.astype(jnp.bfloat16), 'member', axis=0, tiled=True)  62.1 us
    all_gather x1, waiting for transfers between devices, per_device(): proj_full = lax.all_gather(ple_proj[0], 'member', axis=0, tiled=True)  39.7 us
    reduce_scatter x1, waiting for transfers between devices, per_device(): lax.psum_scatter(partial, 'member', scatter_dimension=0, tiled=True)  39.6 us
    all_to_all x1, blocking collectives, per_device(): lax.all_to_all(requests, ('group', 'member'), split_axis=0, concat_axis=0...  21.1 us
    all_to_all x1, blocking collectives, per_device(): lax.all_to_all(served, ('group', 'member'), split_axis=0, concat_axis=0,...  14.6 us
    dot_general x1, matrix products, per_device(): jnp.dot(activated, w_down[0], preferred_element_type=jnp.float32)  12.4 us
    unnamed x19, local copies, waits for them, and re-layouts  7.27 us
    dot_general x1, matrix products, per_device(): gate_part = jnp.dot(normed, w_gate[0], preferred_element_type=jnp.float32)  6.81 us
  transfers between devices with their start and end apart: 4, of which 3 were waited for; matrix products, arithmetic and copies ran while one was open for 7% of the time, Pallas kernels for 0%

profile of v1, /device:TPU:1, one launch (start us, length us, event | category | flops | bytes accessed | tf_op | source)
XLA Modules:
  0.0 246.0 jit_solution(4342978858987168150)
XLA Ops:
  6.5 4.2 %fusion = f32[1536]{0:T(1024)S(1)} fusion(bf16[1536,2048]{1,0:T(8,128)(2,1)} %param.11), kind=kLoop, calls=%fused_computation.3 | loop fusion | flops 9435648 | bytes 6297600 | tf_op jit(solution)/shard_map/reduce_sum | solution.py:11
  10.8 0.5 copy-done.2
  11.3 6.8 %fusion.13 = f32[1536,512]{1,0:T(8,128)} fusion(bf16[1,2048,512]{2,1,0:T(8,128)(2,1)} %param.17, bf16[1536,2048]{1,0:T(8,128)(2,1)S(1)} %copy-done.2, f32[2048]{0:T(1024)S(1)} %bitcast.38, f32[1536]{0:T(1024)S(1)} %add_rsqrt_fusion), kind=kOutput, calls=%fused_computation.19 | convolution fusion | flops 3233808384 | bytes 11548672 | tf_op jit(solution)/shard_map/dot_general | solution.py:39
  18.1 12.4 %convolution_convert_fusion = bf16[1536,2048]{1,0:T(8,128)(2,1)} fusion(bf16[1,512,2048]{2,1,0:T(8,128)(2,1)S(1)} %copy-done, f32[1536,512]{1,0:T(8,128)} %fusion.13, bf16[1,2048,512]{2,1,0:T(8,128)(2,1)} %param.18, bf16[1536,2048]{1,0:T(8,128)(2,1)} %param.11, f32[2048]{0:T(1024)S(1)} %bitcast.39, f32[1536]{0:T(1024)S(1)} %add_rsqrt_fusion), kind=kOutput, calls=%fused_computation.6 | convolution fusion | flops 6466043904 | bytes 19937280 | tf_op jit(solution)/shard_map/dot_general | solution.py:42
  30.6 0.7 all-gather.6.cloned.1.call-update
  31.3 1.2 gather_fusion
  32.6 0.2 convert_reduce_fusion
  32.8 2.7 %select_reduce_fusion = (s32[128,2]{1,0:T(8,128)S(1)}, pred[96,128,2]{0,2,1:T(4,128)(4,1)}) fusion(s32[96]{0:T(128)S(1)} %broadcast_add_fusion, pred[96,2]{0,1:T(4,128)(4,1)S(1)} %iota_compare_fusion.6, pred[96,128]{0,1:T(8,128)(4,1)S(1)} %iota_compare_fusion.4), kind=kLoop, calls=%fused_computation.43 | loop fusion | flops 73472 | bytes 38464 | tf_op jit(solution)/shard_map/reduce_sum | solution.py:53
  35.5 21.1 %all_to_all.24 = s32[128,1,2]{2,1,0:T(1,128)S(1)} all-to-all(s32[128,1,2]{2,1,0:T(1,128)S(1)} %bitcast.33), channel_id=1, replica_groups=mesh['group'=8,'member'=16] {'group','member'}, dimensions={0} | all-to-all | bytes 2048 | tf_op jit(solution)/shard_map/all_to_all | solution.py:54
  56.5 0.2 add_reduce_fusion
  56.7 0.1 sub.7
  56.9 1.7 fusion.22
  58.6 0.1 all_to_all.20
  58.7 0.6 broadcast.111
  59.3 1.4 reduce.5
  60.7 14.6 %all_to_all.25 = bf16[128,2,256]{2,1,0:T(2,128)(2,1)S(1)} all-to-all(bf16[128,2,256]{2,1,0:T(2,128)(2,1)S(1)} %reshape.133), channel_id=1, replica_groups=mesh['group'=8,'member'=16] {'group','member'}, dimensions={0} | all-to-all | bytes 262144 | tf_op jit(solution)/shard_map/all_to_all | solution.py:63
  75.4 1.2 stack.2
  76.5 3.7 %all-to-all-start = ((bf16[16,16,2048]{2,1,0:T(8,128)(2,1)}), bf16[16,16,2048]{2,1,0:T(8,128)(2,1)S(1)}, u32[]{:S(2)}, u32[]{:S(2)}) async-start(bf16[16,16,2048]{2,1,0:T(8,128)(2,1)} %stack.2), calls=%async_computation.1 | async-start | bytes 2097152 | tf_op jit(solution)/shard_map/all_to_all | solution.py:35
  80.2 0.0 all-gather.4.cloned.1.call-start
  80.2 1.5 and.31
  81.8 0.1 reshape.134
  81.9 0.8 reduce.1
  82.6 0.7 reshape.115
  83.3 39.6 %reduce-scatter.2.cloned.1.call-done = bf16[96,2048]{1,0:T(8,128)(2,1)} async-done(((bf16[1536,2048]{1,0:T(8,128)(2,1)}), bf16[96,2048]{1,0:T(8,128)(2,1)}) %reduce-scatter.2.cloned.1.call-update) | async-done | bytes 393232 | tf_op jit(solution)/shard_map/reduce_scatter | solution.py:43
  122.9 1.2 fusion.28
  124.2 0.5 add_rsqrt_fusion.2
  124.7 2.3 fusion.43
  127.0 39.7 %all-gather.6.cloned.1.call-done = bf16[1,256,2048]{2,1,0:T(8,128)(2,1)} async-done(((bf16[1,16,2048]{2,1,0:T(8,128)(2,1)}), bf16[1,256,2048]{2,1,0:T(8,128)(2,1)}) %all-gather.6.cloned.1.call-update) | async-done | bytes 1048592 | tf_op jit(solution)/shard_map/all_gather | solution.py:37
  166.7 2.0 multiply_reduce_fusion
  168.7 2.1 add_convert_fusion
  170.8 62.1 %all-gather.4.cloned.1.call-done = bf16[1536,2048]{1,0:T(8,128)(2,1)} async-done(((bf16[96,2048]{1,0:T(8,128)(2,1)}), bf16[1536,2048]{1,0:T(8,128)(2,1)}) %all-gather.4.cloned.1.call-update) | async-done | bytes 6291472 | tf_op jit(solution)/shard_map/all_gather | solution.py:79
  232.9 6.6 %copy.17 = bf16[1536,2048]{1,0:T(8,128)(2,1)} copy(bf16[1536,2048]{1,0:T(8,128)(2,1)} %all-gather.4.cloned.1.call-done) | data formatting | bytes 12582912
  (29 shorter events, 0.2 us)
Async XLA Ops:
  6.5 11.6 %copy-start = (bf16[1,512,2048]{2,1,0:T(8,128)(2,1)S(1)}, bf16[1,512,2048]{2,1,0:T(8,128)(2,1)}, u32[]{:S(2)}) copy-start(bf16[1,512,2048]{2,1,0:T(8,128)(2,1)} %param.19) | copy-start | bytes 6291460
  6.5 4.3 %copy-start.5 = (f32[1,3,2048]{2,0,1:T(1,128)S(1)}, f32[1,3,2048]{2,0,1:T(1,128)}, u32[]{:S(2)}) copy-start(f32[1,3,2048]{2,0,1:T(1,128)} %param.16) | copy-start | bytes 73732
  6.5 116.4 %reduce-scatter.2.cloned.1.call-start = ((), (), s32[]{:S(2)}) async-start(), calls=%async_computation.4 | async-start | bytes 6684672 | tf_op jit(solution)/shard_map/reduce_scatter | solution.py:43
  6.5 4.8 %copy-start.2 = (bf16[1536,2048]{1,0:T(8,128)(2,1)S(1)}, bf16[1536,2048]{1,0:T(8,128)(2,1)}, u32[]{:S(2)}) copy-start(bf16[1536,2048]{1,0:T(8,128)(2,1)} %param.11) | copy-start | bytes 18874372
  30.5 0.8 copy-start.6
  30.5 0.8 copy-start.1
  30.5 2.3 copy-start.7
  30.5 44.9 %copy-start.4 = (bf16[1,2048,16]{1,2,0:T(8,128)(2,1)S(1)}, bf16[1,2048,16]{1,2,0:T(8,128)(2,1)}, u32[]{:S(2)}) copy-start(bf16[1,2048,16]{1,2,0:T(8,128)(2,1)} %param.20) | copy-start | bytes 196612
  30.5 136.2 %all-gather.6.cloned.1.call-start = ((), (), s32[]{:S(2)}) async-start(), calls=%async_computation.6 | async-start | bytes 1114112 | tf_op jit(solution)/shard_map/all_gather | solution.py:37
  76.5 48.2 %all-to-all-start = ((bf16[16,16,2048]{2,1,0:T(8,128)(2,1)}), bf16[16,16,2048]{2,1,0:T(8,128)(2,1)S(1)}, u32[]{:S(2)}, u32[]{:S(2)}) async-start(bf16[16,16,2048]{2,1,0:T(8,128)(2,1)} %stack.2), calls=%async_computation.1 | async-start | bytes 2097152 | tf_op jit(solution)/shard_map/all_to_all | solution.py:35
  80.2 152.7 %all-gather.4.cloned.1.call-start = ((), (), s32[]{:S(2)}) async-start(), calls=%async_computation.5 | async-start | bytes 6684672 | tf_op jit(solution)/shard_map/all_gather | solution.py:79
  122.9 45.7 %copy-start.3 = (bf16[96,2048]{1,0:T(8,128)(2,1)S(1)}, bf16[96,2048]{1,0:T(8,128)(2,1)}, u32[]{:S(2)}) copy-start(bf16[96,2048]{1,0:T(8,128)(2,1)} %reduce-scatter.2.cloned.1.call-done) | copy-start | bytes 1179652
Sparse Core Ops, SparseCore 0:
  30.6 92.2 reduce-scatter.1
  125.1 41.5 all-gather.5
  170.9 61.9 all-gather.3
